TPU v7x, 32 devices: a whole 2x2x4 slice. The times are simulated.
32 devices in a mesh: parts: 2 (over y), wide: 4 (over z), rep: 2 (over x), sub: 2 (over core).
Axes of the slice: x: 2, y: 2, z: 4, core: 2. Of those that a mesh axis runs over, the one named last changes fastest.
Arguments:
- activations: bfloat16 [8, 2048, 512], P(('parts', 'wide'), 'sub'), parts along dimension 0, may hold values from -6 to 6
- deltas: bfloat16 [8, 2048, 512], P(('parts', 'wide'), 'sub'), parts along dimension 0, may hold values from -6 to 6
- act_factor: bfloat16 [512, 512], P(None, 'rep'), as said below
- delta_factor: bfloat16 [512, 512], P(None, 'rep'), as said below
- queries: bfloat16 [1280, 512, 512], P(None, ('rep', 'wide'), 'sub'), may hold values from -0.00059890747 to 0.00059890747
- assignment: int32 [8], P('parts'), parts along dimension 0, may hold values from 0 to 3, each once
- padding: int32 [8], P(('parts', 'wide')), parts along dimension 0, may hold values from 0 to 1023
Outputs:
- scores: float32 [8, 1280], P(('parts', 'wide'), ('rep', 'sub')), parts along dimension 0
There are 2 independent parts, one for each index of `parts`. A program takes and returns all parts, laid end to end along the dimension named above; an argument that names none is the same for every part. Nothing has to cross between parts.
Inputs may be any that keep to these rules, and one draw needn't show every extreme that they name: `act_factor`: symmetric and positive definite. `delta_factor`: symmetric and positive definite. `assignment`: each number once.
All inputs are finite; a program needn't handle non-finite values.
Results may differ from a plain program's by a relative error of at most 0.005.
Values may be sent and summed in bfloat16 or wider, within the bound.
A program may use at most 128 MiB of HBM per device.

v0:
```python
import functools

import jax
import jax.numpy as jnp
from jax import lax
from jax.experimental import pallas as pl
from jax.experimental.pallas import tpu as pltpu
from jax.sharding import PartitionSpec as P

MESH = pl.DeviceIdType.MESH
GROUP = 160


def general_shards(
    activations, deltas, act_factor, delta_factor, queries, assignment, padding
):
    seq_dev, tok_dev, feature_width = activations.shape
    full_length = tok_dev * lax.axis_size("sub")
    token_start = lax.axis_index("sub") * tok_dev
    positions = token_start + lax.broadcasted_iota(jnp.int32, (seq_dev, tok_dev), 1)
    kept_mask = positions < (full_length - padding)[:, None]
    masked = jnp.where(kept_mask[:, :, None], deltas, jnp.zeros((), jnp.bfloat16))
    delta_proj = jnp.einsum(
        "stw,wi->sti", masked, delta_factor, preferred_element_type=jnp.float32
    ).astype(jnp.bfloat16)
    act_proj = jnp.einsum(
        "stw,wj->stj",
        activations,
        lax.all_gather(act_factor, "rep", axis=1, tiled=True),
        preferred_element_type=jnp.float32,
    ).astype(jnp.bfloat16)
    partial_value = jnp.einsum(
        "sti,stj->sij", delta_proj, act_proj, preferred_element_type=jnp.float32
    )
    summed = lax.psum_scatter(partial_value, "sub", scatter_dimension=2, tiled=True).astype(
        jnp.bfloat16
    )
    regrouped = lax.all_to_all(summed, "wide", split_axis=1, concat_axis=0, tiled=True)
    seq_total = regrouped.shape[0]
    grad_rows = regrouped.reshape(seq_total, -1)
    query_rows = queries.reshape(queries.shape[0], -1)
    partial_scores = lax.dot_general(
        grad_rows, query_rows, (((1,), (1,)), ((), ())), preferred_element_type=jnp.float32
    )
    inverse_order = (
        jnp.zeros((seq_total,), jnp.int32)
        .at[assignment]
        .set(jnp.arange(seq_total, dtype=jnp.int32))
    )
    ranked = jnp.take(partial_scores, inverse_order, axis=0)
    by_column = lax.psum_scatter(ranked, ("rep", "sub"), scatter_dimension=1, tiled=True)
    return lax.psum_scatter(by_column, "wide", scatter_dimension=0, tiled=True)


def kernel(
    n_wide,
    rows,
    assignment_ref,
    padding_ref,
    act_hbm,
    delta_hbm,
    act_factor_hbm,
    delta_factor_hbm,
    query_hbm,
    out_ref,
    act,
    delta,
    act_factor,
    delta_factor,
    query,
    diag,
    inner_mine,
    inner_theirs,
    factor_cols,
    grad,
    grad_all,
    weights,
    folded,
    outgoing,
    incoming,
    load_sem,
    query_sem,
    diag_sem,
    inner_sem,
    grad_send_sem,
    grad_recv_sem,
    score_send_sem,
    score_recv_sem,
):
    z = lax.axis_index("wide")
    r = lax.axis_index("rep")
    c = lax.axis_index("sub")
    n_rep, n_sub = 2, 2

    def peer(dz, dr, dc):
        return {
            "wide": lax.rem(z + dz, n_wide),
            "rep": lax.rem(r + dr, n_rep),
            "sub": lax.rem(c + dc, n_sub),
        }

    block_order = ((1, 1), (1, 0), (0, 1), (0, 0))
    everyone = [(0, 0, 1), (0, 1, 0)] + [(dz, 0, 0) for dz in range(n_wide - 1, 0, -1)]
    barrier = pltpu.get_barrier_semaphore()
    for offset in everyone:
        pl.semaphore_signal(barrier, inc=1, device_id=peer(*offset), device_id_type=MESH)

    loads = [
        pltpu.make_async_copy(src, dst, load_sem.at[k])
        for k, (src, dst) in enumerate(
            (
                (delta_factor_hbm, delta_factor),
                (delta_hbm, delta),
                (act_factor_hbm, act_factor),
                (act_hbm, act),
            )
        )
    ]
    for load in loads:
        load.start()

    chunk = GROUP * rows
    total = query.shape[0]
    block_groups = total // (chunk * n_rep * n_sub)

    def query_copy(place):
        span = pl.ds(pl.multiple_of(place * chunk, chunk), chunk)
        return pltpu.make_async_copy(query_hbm.at[span, :], query.at[span, :], query_sem.at[place])

    def block_at(dr, dc):
        return lax.rem(r + dr, n_rep) * n_sub + lax.rem(c + dc, n_sub)

    half = act_factor.shape[1]
    pl.semaphore_wait(barrier, len(everyone))
    diag_rows = pl.ds(pl.multiple_of(c * half, half), half)
    diag_copy = pltpu.make_async_remote_copy(
        src_ref=act_factor_hbm.at[diag_rows, :],
        dst_ref=diag,
        send_sem=diag_sem.at[0],
        recv_sem=diag_sem.at[1],
        device_id=peer(0, 1, 0),
        device_id_type=MESH,
    )

    @pl.when(r == c)
    def _():
        diag_copy.start()

    loads[0].wait()
    loads[1].wait()
    tokens = delta.shape[0]
    limit = n_sub * tokens - padding_ref[0] - c * tokens
    position = lax.broadcasted_iota(jnp.int32, (tokens, half), 0)
    projected = jnp.dot(delta[...], delta_factor[...], preferred_element_type=jnp.float32)
    delta_proj = jnp.where(position < limit, projected, 0.0).astype(jnp.bfloat16)

    loads[2].wait()
    loads[3].wait()
    for dr, dc in block_order:
        first = block_at(dr, dc) * block_groups

        def begin(t, carry, first=first):
            query_copy(first + t).start()
            return carry

        lax.fori_loop(0, block_groups, begin, 0)

    inner_mine[...] = lax.dot_general(
        delta_proj, act[...], (((0,), (0,)), ((), ())), preferred_element_type=jnp.float32
    )
    inner_copy = pltpu.make_async_remote_copy(
        src_ref=inner_mine,
        dst_ref=inner_theirs,
        send_sem=inner_sem.at[0],
        recv_sem=inner_sem.at[1],
        device_id=peer(0, 0, 1),
        device_id_type=MESH,
    )
    inner_copy.start()

    @pl.when(r == c)
    def _():
        factor_cols[...] = act_factor[...]
        diag_copy.wait_send()

    @pl.when(r != c)
    def _():
        mirrored = act_factor[diag_rows, :].astype(jnp.float32).T.astype(jnp.bfloat16)
        factor_cols[pl.ds(pl.multiple_of(r * half, half), half), :] = mirrored
        diag_copy.wait_recv()
        factor_cols[diag_rows, :] = diag[...]

    inner_copy.wait_recv()
    inner = inner_mine[...] + inner_theirs[...]
    high = inner.astype(jnp.bfloat16)
    low = (inner - high.astype(jnp.float32)).astype(jnp.bfloat16)
    gradient = jnp.dot(high, factor_cols[...], preferred_element_type=jnp.float32) + jnp.dot(
        low, factor_cols[...], preferred_element_type=jnp.float32
    )
    grad[...] = gradient.astype(jnp.bfloat16)
    mine = pl.ds(pl.multiple_of(z * rows, rows), rows)
    grad_copies = []
    for dz in range(n_wide - 1, 0, -1):
        target = pl.ds(pl.multiple_of(lax.rem(z + dz, n_wide) * rows, rows), rows)
        copy = pltpu.make_async_remote_copy(
            src_ref=grad.at[target, :],
            dst_ref=grad_all.at[mine, :],
            send_sem=grad_send_sem.at[dz],
            recv_sem=grad_recv_sem.at[dz],
            device_id=peer(dz, 0, 0),
            device_id_type=MESH,
        )
        copy.start()
        grad_copies.append(copy)
    grad_all[mine, :] = grad[mine, :]

    width = n_wide * rows
    lane = lax.broadcasted_iota(jnp.int32, (8, width), 1)
    sublane = lax.broadcasted_iota(jnp.int32, (8, width), 0)
    owner = lane // rows
    ranks = jnp.zeros((8, width), jnp.int32)
    for n in range(n_wide):
        ranks = jnp.where(owner == n, assignment_ref[n], ranks)
    places = jnp.where(ranks == sublane, 1.0, 0.0).astype(jnp.bfloat16)
    tile_of_lane = lax.rem(lane, rows) // 8
    on_diagonal = lax.rem(lane, 8) == sublane

    block_size = block_groups * GROUP
    folded[pl.ds(block_size, folded.shape[0] - block_size), :] = jnp.zeros(
        (folded.shape[0] - block_size, width), jnp.float32
    )
    inner_copy.wait_send()
    for copy in grad_copies:
        copy.wait_recv()
    weights[...] = grad_all[...].astype(jnp.float32).T.astype(jnp.bfloat16)

    def score_copy(k, dz):
        slot = k * n_wide + dz
        return pltpu.make_async_remote_copy(
            src_ref=outgoing.at[k, lax.rem(z + dz, n_wide)],
            dst_ref=incoming.at[slot],
            send_sem=score_send_sem.at[slot],
            recv_sem=score_recv_sem.at[slot],
            device_id=peer(dz, 1 - k // n_sub, 1 - lax.rem(k, n_sub)),
            device_id_type=MESH,
        )

    last = len(block_order) - 1

    def score_block(k, carry):
        first = block_at(1 - k // n_sub, 1 - lax.rem(k, n_sub)) * block_groups

        def score_group(t, inner_carry):
            query_copy(first + t).wait()
            span = pl.ds(pl.multiple_of((first + t) * chunk, chunk), chunk)
            products = jnp.dot(
                query[span, :], weights[...], preferred_element_type=jnp.float32
            ).reshape(GROUP, rows // 8, 8, width)
            chosen = products[:, 0]
            for a in range(1, rows // 8):
                chosen = jnp.where((tile_of_lane == a)[None], products[:, a], chosen)
            chosen = jnp.where(on_diagonal[None], chosen, 0.0)
            folded[pl.ds(pl.multiple_of(t * GROUP, GROUP), GROUP), :] = jnp.sum(chosen, axis=1)
            return inner_carry

        lax.fori_loop(0, block_groups, score_group, 0)
        sums = folded[...]
        sums_high = sums.astype(jnp.bfloat16)
        sums_low = (sums - sums_high.astype(jnp.float32)).astype(jnp.bfloat16)
        contract = (((1,), (1,)), ((), ()))
        ranked = lax.dot_general(
            places, sums_high, contract, preferred_element_type=jnp.float32
        ) + lax.dot_general(places, sums_low, contract, preferred_element_type=jnp.float32)
        for p in range(n_wide):
            outgoing[k, p] = ranked[p : p + 1, :]
        for dz in range(n_wide - 1, 0, -1):
            score_copy(k, dz).start()

        @pl.when(k < last)
        def _():
            score_copy(k, 0).start()

        return carry

    lax.fori_loop(0, len(block_order), score_block, 0)

    result = outgoing[last, z]
    for copy in grad_copies:
        copy.wait_send()
    for k in range(last + 1):
        for dz in range(n_wide - 1, -1, -1):
            if (k, dz) != (last, 0):
                score_copy(k, dz).wait()
                result = result + incoming[k * n_wide + dz]
    out_ref[...] = result[:, :block_size]


def fused_shards(
    n_wide, activations, deltas, act_factor, delta_factor, queries, assignment, padding
):
    _, tokens, features = activations.shape
    n_queries, rows, columns = queries.shape
    half = act_factor.shape[1]
    width = n_wide * rows
    groups = n_queries // GROUP
    block_size = n_queries // 4
    padded = -(-block_size // 128) * 128
    hbm = pl.BlockSpec(memory_space=pl.ANY)
    smem = pl.BlockSpec(memory_space=pltpu.SMEM)
    dma = pltpu.SemaphoreType.DMA
    bf16, f32 = jnp.bfloat16, jnp.float32
    return pl.pallas_call(
        functools.partial(kernel, n_wide, rows),
        out_shape=jax.ShapeDtypeStruct((1, block_size), f32),
        in_specs=[smem, smem] + [hbm] * 5,
        out_specs=pl.BlockSpec(memory_space=pltpu.VMEM),
        scratch_shapes=[
            pltpu.VMEM((tokens, features), bf16),
            pltpu.VMEM((tokens, features), bf16),
            pltpu.VMEM((features, half), bf16),
            pltpu.VMEM((features, half), bf16),
            pltpu.VMEM((n_queries * rows, columns), bf16),
            pltpu.VMEM((half, half), bf16),
            pltpu.VMEM((half, features), f32),
            pltpu.VMEM((half, features), f32),
            pltpu.VMEM((features, half), bf16),
            pltpu.VMEM((half, columns), bf16),
            pltpu.VMEM((width, columns), bf16),
            pltpu.VMEM((columns, width), bf16),
            pltpu.VMEM((padded, width), f32),
            pltpu.VMEM((4, n_wide, 1, padded), f32),
            pltpu.VMEM((4 * n_wide, 1, padded), f32),
            dma((4,)),
            dma((groups,)),
            dma((2,)),
            dma((2,)),
            dma((n_wide,)),
            dma((n_wide,)),
            dma((4 * n_wide,)),
            dma((4 * n_wide,)),
        ],
        compiler_params=pltpu.CompilerParams(
            collective_id=0, has_side_effects=True, vmem_limit_bytes=60 * 1024 * 1024
        ),
    )(
        assignment,
        padding,
        activations.reshape(tokens, features),
        deltas.reshape(tokens, features),
        act_factor,
        delta_factor,
        queries.reshape(n_queries * rows, columns),
    )


def solution(mesh):
    placed = (
        P(("parts", "wide"), "sub", None),
        P(("parts", "wide"), "sub", None),
        P(None, "rep"),
        P(None, "rep"),
        P(None, ("rep", "wide"), "sub"),
        P("parts"),
        P(("parts", "wide")),
    )
    n_wide, n_rep, n_sub = (mesh.shape[name] for name in ("wide", "rep", "sub"))

    def shards(activations, deltas, act_factor, delta_factor, queries, assignment, padding):
        seq_dev, tokens, features = activations.shape
        n_queries, rows, columns = queries.shape
        fits = (
            seq_dev == 1
            and (n_rep, n_sub) == (2, 2)
            and n_wide <= 8
            and rows % 16 == 0
            and (n_wide * rows) % 128 == 0
            and columns % 128 == 0
            and act_factor.shape[1] == columns == n_wide * rows
            and tokens % 16 == 0
            and n_queries % (4 * GROUP) == 0
            and n_queries * rows * columns * 2 <= 44 * 2**20
        )
        run = functools.partial(fused_shards, n_wide) if fits else general_shards
        return run(activations, deltas, act_factor, delta_factor, queries, assignment, padding)

    return jax.shard_map(
        shards,
        mesh=mesh,
        in_specs=placed,
        out_specs=P(("parts", "wide"), ("rep", "sub")),
        check_vma=False,
    )
```

profile of v0, /device:TPU:0, one launch (start us, length us, event | category | flops | bytes accessed | tf_op | source)
XLA Modules:
  0.0 33.3 jit_solution(17629002265065848258)
XLA Ops:
  0.7 31.4 %shard_map.73 = f32[1,320]{1,0:T(1,128)} custom-call(s32[4]{0:T(128)} %assignment_ref.1, s32[1]{0:T(128)S(6)} %copy.9.padding_ref, bf16[1024,512]{1,0:T(8,128)(2,1)} %bitcast.4, bf16[1024,512]{1,0:T(8,128)(2,1)} %bitcast.5, bf16[512,256]{1,0:T(8,128)(2,1)} %act_factor_hbm.1, bf16[512,256]{1,0:T(8,128)(2,1)} %delta_factor_hbm.1, bf16[81920,256]{1,0:T(8,128)(2,1)} %bitcast.3), custom_call_target="tpu_custom_call" | custom-call | tf_op jit(solution)/shard_map/pallas_call | solution.py:312
  32.1 1.2 %copy.10 = f32[1,320]{1,0:T(1,128)} copy(f32[1,320]{1,0:T(1,128)} %shard_map.73) | data formatting | bytes 2560
where the time goes:
time: 33.5 us; the launch traced here: 33.3 us
  Pallas kernels  31.4 us (94%)
  local copies, waits for them, and re-layouts  1.24 us (4%)
  between operations  0.66 us (2%)
    pallas_call x1, Pallas kernels, fused_shards(): pl.pallas_call(functools.partial(kernel, n_wide, rows), out_shape=jax.Sha...  31.4 us
    unnamed x1, local copies, waits for them, and re-layouts  1.24 us

commit v1 on v0

v1 whole, which is shorter than its diff:
```python
import functools

import jax
import jax.numpy as jnp
from jax import lax
from jax.experimental import pallas as pl
from jax.experimental.pallas import tpu as pltpu
from jax.sharding import PartitionSpec as P

MESH = pl.DeviceIdType.MESH
UNIT = 32
PIECES = 2


def general_shards(
    activations, deltas, act_factor, delta_factor, queries, assignment, padding
):
    seq_dev, tok_dev, feature_width = activations.shape
    full_length = tok_dev * lax.axis_size("sub")
    token_start = lax.axis_index("sub") * tok_dev
    positions = token_start + lax.broadcasted_iota(jnp.int32, (seq_dev, tok_dev), 1)
    kept_mask = positions < (full_length - padding)[:, None]
    masked = jnp.where(kept_mask[:, :, None], deltas, jnp.zeros((), jnp.bfloat16))
    delta_proj = jnp.einsum(
        "stw,wi->sti", masked, delta_factor, preferred_element_type=jnp.float32
    ).astype(jnp.bfloat16)
    act_proj = jnp.einsum(
        "stw,wj->stj",
        activations,
        lax.all_gather(act_factor, "rep", axis=1, tiled=True),
        preferred_element_type=jnp.float32,
    ).astype(jnp.bfloat16)
    partial_value = jnp.einsum(
        "sti,stj->sij", delta_proj, act_proj, preferred_element_type=jnp.float32
    )
    summed = lax.psum_scatter(partial_value, "sub", scatter_dimension=2, tiled=True).astype(
        jnp.bfloat16
    )
    regrouped = lax.all_to_all(summed, "wide", split_axis=1, concat_axis=0, tiled=True)
    seq_total = regrouped.shape[0]
    grad_rows = regrouped.reshape(seq_total, -1)
    query_rows = queries.reshape(queries.shape[0], -1)
    partial_scores = lax.dot_general(
        grad_rows, query_rows, (((1,), (1,)), ((), ())), preferred_element_type=jnp.float32
    )
    inverse_order = (
        jnp.zeros((seq_total,), jnp.int32)
        .at[assignment]
        .set(jnp.arange(seq_total, dtype=jnp.int32))
    )
    ranked = jnp.take(partial_scores, inverse_order, axis=0)
    by_column = lax.psum_scatter(ranked, ("rep", "sub"), scatter_dimension=1, tiled=True)
    return lax.psum_scatter(by_column, "wide", scatter_dimension=0, tiled=True)


def kernel(
    n_wide,
    pieces,
    assignment_hbm,
    padding_hbm,
    act_hbm,
    delta_hbm,
    act_factor_hbm,
    delta_factor_hbm,
    query_hbm,
    out_ref,
    assignment,
    padding,
    act,
    delta,
    act_factor,
    delta_factor,
    query,
    diag,
    inner_mine,
    inner_theirs,
    factor_cols,
    grad,
    grad_all,
    total_wide,
    total_tall,
    outgoing,
    incoming,
    ready_sem,
    load_sem,
    query_sem,
    diag_sem,
    inner_send_sem,
    inner_recv_sem,
    grad_send_sem,
    grad_recv_sem,
    score_send_sem,
    score_recv_sem,
):
    z = lax.axis_index("wide")
    r = lax.axis_index("rep")
    c = lax.axis_index("sub")
    n_queries, rows, columns = query.shape
    depth = rows // pieces
    block_size = n_queries // 4
    pair = 2 * block_size
    f32, bf16 = jnp.float32, jnp.bfloat16

    def peer(dz, dr, dc):
        return {
            "wide": lax.rem(z + dz, n_wide),
            "rep": lax.rem(r + dr, 2),
            "sub": lax.rem(c + dc, 2),
        }

    def signal_wide(sem, place):
        pl.semaphore_signal(sem, inc=1, device_id={"wide": place}, device_id_type=MESH)

    barrier = pltpu.get_barrier_semaphore()
    for offset in ((0, 0, 1), (0, 1, 0)):
        pl.semaphore_signal(barrier, inc=1, device_id=peer(*offset), device_id_type=MESH)
    has_below, has_above = z > 0, z < n_wide - 1

    @pl.when(has_below)
    def _():
        signal_wide(barrier, z - 1)

    @pl.when(has_above)
    def _():
        signal_wide(barrier, z + 1)

    loads = [
        pltpu.make_async_copy(src, dst, load_sem.at[k])
        for k, (src, dst) in enumerate(
            (
                (padding_hbm, padding),
                (delta_factor_hbm, delta_factor),
                (delta_hbm, delta),
                (act_hbm, act),
                (act_factor_hbm, act_factor),
                (assignment_hbm, assignment),
            )
        )
    ]
    for load in loads:
        load.start()

    def query_copy(piece, block):
        span = pl.ds(pl.multiple_of(block * block_size, block_size), block_size)
        part = pl.ds(piece * depth, depth)
        return pltpu.make_async_copy(
            query_hbm.at[span, part, :], query.at[span, part, :], query_sem.at[piece * 4 + block]
        )

    half = act_factor.shape[1]
    pl.semaphore_wait(barrier, 2 + has_below.astype(jnp.int32) + has_above.astype(jnp.int32))

    @pl.when(has_below & has_above)
    def _():
        signal_wide(ready_sem.at[z + 1], z - 1)
        signal_wide(ready_sem.at[z - 1], z + 1)

    diag_rows = pl.ds(pl.multiple_of(c * half, half), half)
    diag_copy = pltpu.make_async_remote_copy(
        src_ref=act_factor_hbm.at[diag_rows, :],
        dst_ref=diag,
        send_sem=diag_sem.at[0],
        recv_sem=diag_sem.at[1],
        device_id=peer(0, 1, 0),
        device_id_type=MESH,
    )

    @pl.when(r == c)
    def _():
        diag_copy.start()

    for load in loads[:3]:
        load.wait()
    for piece in range(pieces):
        for block in range(4):
            query_copy(piece, block).start()
    tokens = delta.shape[0]
    limit = 2 * tokens - padding[0] - c * tokens
    position = lax.broadcasted_iota(jnp.int32, (tokens, half), 0)
    projected = jnp.dot(delta[...], delta_factor[...], preferred_element_type=f32)
    delta_proj = jnp.where(position < limit, projected, 0.0).astype(bf16)

    loads[3].wait()
    loads[4].wait()
    inner = lax.dot_general(
        delta_proj, act[...], (((0,), (0,)), ((), ())), preferred_element_type=f32
    )
    inner_copies = []
    for s in range(pieces):
        for p in range(n_wide):
            first = p * rows + s * depth
            inner_mine[s, p * depth : (p + 1) * depth, :] = inner[first : first + depth, :]
        copy = pltpu.make_async_remote_copy(
            src_ref=inner_mine.at[s],
            dst_ref=inner_theirs.at[s],
            send_sem=inner_send_sem.at[s],
            recv_sem=inner_recv_sem.at[s],
            device_id=peer(0, 0, 1),
            device_id_type=MESH,
        )
        copy.start()
        inner_copies.append(copy)

    for d in range(2, n_wide):

        @pl.when(z + d < n_wide)
        def _(d=d):
            pl.semaphore_wait(ready_sem.at[z + d], 1)

        @pl.when((z + d < n_wide) & has_below)
        def _(d=d):
            signal_wide(ready_sem.at[z + d], z - 1)

        @pl.when(z - d >= 0)
        def _(d=d):
            pl.semaphore_wait(ready_sem.at[z - d], 1)

        @pl.when((z - d >= 0) & has_above)
        def _(d=d):
            signal_wide(ready_sem.at[z - d], z + 1)

    @pl.when(r == c)
    def _():
        factor_cols[...] = act_factor[...]

    @pl.when(r != c)
    def _():
        mirrored = act_factor[diag_rows, :].astype(f32).T.astype(bf16)
        factor_cols[pl.ds(pl.multiple_of(r * half, half), half), :] = mirrored
        diag_copy.wait_recv()
        factor_cols[diag_rows, :] = diag[...]

    def grad_copy(s, source, place):
        target = pl.ds(pl.multiple_of(place * depth, depth), depth)
        return pltpu.make_async_remote_copy(
            src_ref=grad.at[s, target, :],
            dst_ref=grad_all.at[source, pl.ds(s * depth, depth), :],
            send_sem=grad_send_sem.at[s * n_wide + place],
            recv_sem=grad_recv_sem.at[s * n_wide + source],
            device_id={"wide": place},
            device_id_type=MESH,
        )

    def others():
        for step in range(n_wide - 1):
            low = n_wide - 1 - step
            yield jnp.where(2 * z < n_wide, low - (low <= z), step + (step >= z))

    for s in range(pieces):
        inner_copies[s].wait_recv()
        both = inner_mine[s] + inner_theirs[s]
        high = both.astype(bf16)
        low = (both - high.astype(f32)).astype(bf16)
        gradient = jnp.dot(high, factor_cols[...], preferred_element_type=f32) + jnp.dot(
            low, factor_cols[...], preferred_element_type=f32
        )
        grad[s] = gradient.astype(bf16)
        for place in others():
            grad_copy(s, z, place).start()
        own = pl.ds(pl.multiple_of(z * depth, depth), depth)
        grad_all[z, s * depth : (s + 1) * depth, :] = grad[s, own, :]

    loads[5].wait()
    stack = 8 * n_wide
    place_lane = lax.broadcasted_iota(jnp.int32, (8, stack), 1) // 8
    ranks = jnp.zeros((8, stack), jnp.int32)
    for n in range(n_wide):
        ranks = jnp.where(place_lane == n, assignment[n], ranks)
    rank_rows = lax.broadcasted_iota(jnp.int32, (8, stack), 0)
    places = jnp.where(ranks == rank_rows, 1.0, 0.0).astype(bf16)
    segments = block_size // 16
    gather = jnp.where(
        lax.broadcasted_iota(jnp.int32, (128, block_size), 0) // 8
        == lax.rem(lax.broadcasted_iota(jnp.int32, (128, block_size), 1), 16),
        1.0,
        0.0,
    ).astype(bf16)
    segment_of_lane = lax.broadcasted_iota(jnp.int32, (8, block_size), 1) // 16
    contract = (((1,), (1,)), ((), ()))

    def split(values):
        high = values.astype(bf16)
        return high, (values - high.astype(f32)).astype(bf16)

    def matches(shape, row_axis, lane_axis):
        return lax.rem(lax.broadcasted_iota(jnp.int32, shape, row_axis), 8) == lax.rem(
            lax.broadcasted_iota(jnp.int32, shape, lane_axis), 8
        )

    def weights(a):
        return grad_all[:, 8 * a : 8 * a + 8, :].reshape(stack, columns)

    def tile(start, a):
        span = pl.ds(pl.multiple_of(start, UNIT), UNIT)
        return query[span, 8 * a : 8 * a + 8, :].reshape(8 * UNIT, columns)

    units = block_size // UNIT

    def contractions(s, base):
        wide, tall = [], []
        for first in range(0, units, 2):
            group = range(first, min(units, first + 2))
            got_wide, got_tall = {}, {}
            for a in range(s * depth // 8, (s + 1) * depth // 8):
                for u in group:
                    term = lax.dot_general(
                        weights(a),
                        tile(base + u * UNIT, a),
                        contract,
                        preferred_element_type=f32,
                    )
                    got_wide[u] = got_wide[u] + term if u in got_wide else term
                for u in group:
                    term = lax.dot_general(
                        tile(base + block_size + u * UNIT, a),
                        weights(a),
                        contract,
                        preferred_element_type=f32,
                    )
                    got_tall[u] = got_tall[u] + term if u in got_tall else term
            wide += [got_wide[u] for u in group]
            tall += [got_tall[u] for u in group]
        return wide, tall

    def wait_queries(s, k):
        for block in range(2):
            query_copy(s, 2 * k + block).wait()

    def wait_grads(s):
        for dz in range(1, n_wide):
            grad_copy(s, lax.rem(z + dz, n_wide), z).wait_recv()

    for s in range(pieces - 1):
        wait_grads(s)

        def add_pair(k, carry, s=s):
            wait_queries(s, k)
            wide, tall = contractions(s, k * pair)
            for u in range(units):
                lanes = slice(8 * UNIT * u, 8 * UNIT * (u + 1))
                if s:
                    total_wide[k, :, lanes] += wide[u]
                    total_tall[k, lanes, :] += tall[u]
                else:
                    total_wide[k, :, lanes] = wide[u]
                    total_tall[k, lanes, :] = tall[u]
            return carry

        lax.fori_loop(0, 2, add_pair, 0)

    def device_of(dz, dr, dc):
        where = peer(dz, dr, dc)
        return (where["wide"] * 2 + where["rep"]) * 2 + where["sub"]

    def score_send(k, dz, dc):
        where = {"wide": lax.rem(z + dz, n_wide), "rep": k, "sub": lax.rem(c + dc, 2)}
        return pltpu.make_async_remote_copy(
            src_ref=outgoing.at[k, where["sub"], where["wide"]],
            dst_ref=incoming.at[device_of(0, 0, 0)],
            send_sem=score_send_sem.at[(k * n_wide + dz) * 2 + dc],
            recv_sem=score_recv_sem.at[device_of(0, 0, 0)],
            device_id=where,
            device_id_type=MESH,
        )

    def score_receive(dz, dr, dc):
        slot = device_of(dz, dr, dc)
        return pltpu.make_async_remote_copy(
            src_ref=outgoing.at[0, 0, 0],
            dst_ref=incoming.at[slot],
            send_sem=score_send_sem.at[0],
            recv_sem=score_recv_sem.at[slot],
            device_id=peer(dz, dr, dc),
            device_id_type=MESH,
        )

    final = pieces - 1
    wait_grads(final)

    def score_pair(k, carry):
        wait_queries(final, k)
        wide, tall = contractions(final, k * pair)
        found = []
        for u in range(units):
            lanes = slice(8 * UNIT * u, 8 * UNIT * (u + 1))
            value = wide[u] + total_wide[k, :, lanes] if pieces > 1 else wide[u]
            value = jnp.where(matches(value.shape, 0, 1), value, 0.0)
            high, low = split(value)
            found.append(
                jnp.dot(places, high, preferred_element_type=f32)
                + jnp.dot(places, low, preferred_element_type=f32)
            )
        ranked = jnp.concatenate(found, axis=1)
        stacked = jnp.concatenate(
            [ranked[:, 128 * g : 128 * (g + 1)] for g in range(segments)], axis=0
        )
        high, low = split(stacked)
        spread = jnp.dot(high, gather, preferred_element_type=f32) + jnp.dot(
            low, gather, preferred_element_type=f32
        )
        scores = jnp.zeros((8, block_size), f32)
        for g in range(segments):
            scores = jnp.where(segment_of_lane == g, spread[8 * g : 8 * g + 8], scores)
        for p in range(n_wide):
            outgoing[k, 0, p] = scores[p : p + 1, :]

        sums = []
        for u in range(units):
            lanes = slice(8 * UNIT * u, 8 * UNIT * (u + 1))
            value = tall[u] + total_tall[k, lanes, :] if pieces > 1 else tall[u]
            value = jnp.where(matches(value.shape, 0, 1), value, 0.0)
            sums.append(jnp.sum(value.reshape(UNIT, 8, stack), axis=1))
        high, low = split(jnp.concatenate(sums, axis=0))
        scores = lax.dot_general(
            places, high, contract, preferred_element_type=f32
        ) + lax.dot_general(places, low, contract, preferred_element_type=f32)
        for p in range(n_wide):
            outgoing[k, 1, p] = scores[p : p + 1, :]
        for dz in range(n_wide - 1, 0, -1):
            for dc in (0, 1):
                score_send(k, dz, dc).start()
        score_send(k, 0, 1).start()

        @pl.when(k != r)
        def _():
            score_send(k, 0, 0).start()

        return carry

    lax.fori_loop(0, 2, score_pair, 0)

    @pl.when(r == c)
    def _():
        diag_copy.wait_send()

    for copy in inner_copies:
        copy.wait_send()
    for s in range(pieces):
        for place in others():
            grad_copy(s, z, place).wait_send()
    for k in range(2):
        for dz in range(n_wide):
            for dc in (0, 1):
                if dz or dc:
                    score_send(k, dz, dc).wait_send()

        @pl.when(k != r)
        def _(k=k):
            score_send(k, 0, 0).wait_send()

    result = outgoing[r, c, z]
    for dz in range(n_wide):
        for dr in (0, 1):
            for dc in (0, 1):
                if dz or dr or dc:
                    score_receive(dz, dr, dc).wait_recv()
                    result = result + incoming[device_of(dz, dr, dc)]
    out_ref[...] = result


def fused_shards(
    n_wide, activations, deltas, act_factor, delta_factor, queries, assignment, padding
):
    _, tokens, features = activations.shape
    n_queries, rows, columns = queries.shape
    half = act_factor.shape[1]
    pieces = PIECES
    depth = rows // pieces
    block_size = n_queries // 4
    hbm = pl.BlockSpec(memory_space=pl.ANY)
    dma = pltpu.SemaphoreType.DMA
    bf16, f32 = jnp.bfloat16, jnp.float32
    return pl.pallas_call(
        functools.partial(kernel, n_wide, pieces),
        out_shape=pltpu.VMEM((1, block_size), f32),
        in_specs=[hbm] * 7,
        out_specs=pl.BlockSpec(memory_space=pltpu.VMEM),
        scratch_shapes=[
            pltpu.SMEM((n_wide,), jnp.int32),
            pltpu.SMEM((1,), jnp.int32),
            pltpu.VMEM((tokens, features), bf16),
            pltpu.VMEM((tokens, features), bf16),
            pltpu.VMEM((features, half), bf16),
            pltpu.VMEM((features, half), bf16),
            pltpu.VMEM((n_queries, rows, columns), bf16),
            pltpu.VMEM((half, half), bf16),
            pltpu.VMEM((pieces, n_wide * depth, features), f32),
            pltpu.VMEM((pieces, n_wide * depth, features), f32),
            pltpu.VMEM((features, half), bf16),
            pltpu.VMEM((pieces, n_wide * depth, columns), bf16),
            pltpu.VMEM((n_wide, rows, columns), bf16),
            pltpu.VMEM((2, 8 * n_wide, 8 * block_size), f32),
            pltpu.VMEM((2, 8 * block_size, 8 * n_wide), f32),
            pltpu.VMEM((2, 2, n_wide, 1, block_size), f32),
            pltpu.VMEM((4 * n_wide, 1, block_size), f32),
            pltpu.SemaphoreType.REGULAR((n_wide,)),
            dma((6,)),
            dma((4 * pieces,)),
            dma((2,)),
            dma((pieces,)),
            dma((pieces,)),
            dma((pieces * n_wide,)),
            dma((pieces * n_wide,)),
            dma((4 * n_wide,)),
            dma((4 * n_wide,)),
        ],
        compiler_params=pltpu.CompilerParams(
            collective_id=0, has_side_effects=True, vmem_limit_bytes=60 * 1024 * 1024
        ),
    )(
        assignment,
        padding,
        activations.reshape(tokens, features),
        deltas.reshape(tokens, features),
        act_factor,
        delta_factor,
        queries,
    )


def solution(mesh):
    placed = (
        P(("parts", "wide"), "sub", None),
        P(("parts", "wide"), "sub", None),
        P(None, "rep"),
        P(None, "rep"),
        P(None, ("rep", "wide"), "sub"),
        P("parts"),
        P(("parts", "wide")),
    )
    n_wide, n_rep, n_sub = (mesh.shape[name] for name in ("wide", "rep", "sub"))

    def shards(activations, deltas, act_factor, delta_factor, queries, assignment, padding):
        seq_dev, tokens, features = activations.shape
        n_queries, rows, columns = queries.shape
        fits = (
            seq_dev == 1
            and (n_rep, n_sub) == (2, 2)
            and n_wide <= 8
            and rows % (8 * PIECES) == 0
            and columns % 128 == 0
            and act_factor.shape[1] == columns == n_wide * rows
            and tokens % 16 == 0
            and n_queries % (4 * UNIT) == 0
            and n_queries * rows * columns * 2 <= 44 * 2**20
        )
        run = functools.partial(fused_shards, n_wide) if fits else general_shards
        return run(activations, deltas, act_factor, delta_factor, queries, assignment, padding)

    return jax.shard_map(
        shards,
        mesh=mesh,
        in_specs=placed,
        out_specs=P(("parts", "wide"), ("rep", "sub")),
        check_vma=False,
    )
```

time: 33.5 us -> 25.1 us (0.75)
  the two profiles are of different devices: /device:TPU:0 before, /device:TPU:3 now
where the time goes in v1:
time: 25.1 us; the launch traced here: 25 us
  Pallas kernels  23.7 us (94%)
  between operations  0.66 us (3%)
  local copies, waits for them, and re-layouts  0.56 us (2%)
    pallas_call x1, Pallas kernels, fused_shards(): pl.pallas_call(functools.partial(kernel, n_wide, pieces), out_shape=pltpu...  23.7 us
    unnamed x1, local copies, waits for them, and re-layouts  0.56 us

profile of v1, /device:TPU:3, one launch (start us, length us, event | category | flops | bytes accessed | tf_op | source)
XLA Modules:
  0.0 25.0 jit_solution(3840963960897708951)
XLA Ops:
  0.7 23.7 %shard_map.73 = f32[1,320]{1,0:T(1,128)S(1)} custom-call(s32[4]{0:T(128)} %assignment_hbm.1, s32[1]{0:T(128)S(6)} %copy.10.padding_hbm, bf16[1024,512]{1,0:T(8,128)(2,1)} %bitcast.2, bf16[1024,512]{1,0:T(8,128)(2,1)} %bitcast.3, bf16[512,256]{1,0:T(8,128)(2,1)} %act_factor_hbm.1, bf16[512,256]{1,0:T(8,128)(2,1)} %delta_factor_hbm.1, ...), custom_call_target="tpu_custom_call" | custom-call | tf_op jit(solution)/shard_map/pallas_call | solution.py:473
  24.4 0.6 %copy.9 = f32[1,320]{1,0:T(1,128)} copy(f32[1,320]{1,0:T(1,128)S(1)} %shard_map.73) | data formatting | bytes 2560

commit v2 on v1

v2 whole, which is shorter than its diff:
```python
import functools

import jax
import jax.numpy as jnp
from jax import lax
from jax.experimental import pallas as pl
from jax.experimental.pallas import tpu as pltpu
from jax.sharding import PartitionSpec as P

MESH = pl.DeviceIdType.MESH
UNIT = 32
PIECES = 2
EARLY = 1
SPLIT = 6


def general_shards(
    activations, deltas, act_factor, delta_factor, queries, assignment, padding
):
    seq_dev, tok_dev, feature_width = activations.shape
    full_length = tok_dev * lax.axis_size("sub")
    token_start = lax.axis_index("sub") * tok_dev
    positions = token_start + lax.broadcasted_iota(jnp.int32, (seq_dev, tok_dev), 1)
    kept_mask = positions < (full_length - padding)[:, None]
    masked = jnp.where(kept_mask[:, :, None], deltas, jnp.zeros((), jnp.bfloat16))
    delta_proj = jnp.einsum(
        "stw,wi->sti", masked, delta_factor, preferred_element_type=jnp.float32
    ).astype(jnp.bfloat16)
    act_proj = jnp.einsum(
        "stw,wj->stj",
        activations,
        lax.all_gather(act_factor, "rep", axis=1, tiled=True),
        preferred_element_type=jnp.float32,
    ).astype(jnp.bfloat16)
    partial_value = jnp.einsum(
        "sti,stj->sij", delta_proj, act_proj, preferred_element_type=jnp.float32
    )
    summed = lax.psum_scatter(partial_value, "sub", scatter_dimension=2, tiled=True).astype(
        jnp.bfloat16
    )
    regrouped = lax.all_to_all(summed, "wide", split_axis=1, concat_axis=0, tiled=True)
    seq_total = regrouped.shape[0]
    grad_rows = regrouped.reshape(seq_total, -1)
    query_rows = queries.reshape(queries.shape[0], -1)
    partial_scores = lax.dot_general(
        grad_rows, query_rows, (((1,), (1,)), ((), ())), preferred_element_type=jnp.float32
    )
    inverse_order = (
        jnp.zeros((seq_total,), jnp.int32)
        .at[assignment]
        .set(jnp.arange(seq_total, dtype=jnp.int32))
    )
    ranked = jnp.take(partial_scores, inverse_order, axis=0)
    by_column = lax.psum_scatter(ranked, ("rep", "sub"), scatter_dimension=1, tiled=True)
    return lax.psum_scatter(by_column, "wide", scatter_dimension=0, tiled=True)


def kernel(
    n_wide,
    pieces,
    assignment_hbm,
    padding_hbm,
    act_hbm,
    delta_hbm,
    act_factor_hbm,
    delta_factor_hbm,
    query_hbm,
    out_ref,
    assignment,
    padding,
    act,
    delta,
    act_factor,
    delta_factor,
    query,
    diag,
    inner_mine,
    inner_sent,
    inner_theirs,
    factor_near,
    factor_far,
    grad_near,
    grad,
    grad_all,
    total_wide,
    total_tall,
    wide_high,
    wide_low,
    stacked,
    tall_sums,
    outgoing,
    incoming,
    ready_sem,
    load_sem,
    query_sem,
    diag_sem,
    inner_send_sem,
    inner_recv_sem,
    grad_send_sem,
    grad_recv_sem,
    score_send_sem,
    score_recv_sem,
):
    z = lax.axis_index("wide")
    r = lax.axis_index("rep")
    c = lax.axis_index("sub")
    n_queries, rows, columns = query.shape
    depth = rows // pieces
    block_size = n_queries // 4
    pair = 2 * block_size
    f32, bf16 = jnp.float32, jnp.bfloat16

    def peer(dz, dr, dc):
        return {
            "wide": lax.rem(z + dz, n_wide),
            "rep": lax.rem(r + dr, 2),
            "sub": lax.rem(c + dc, 2),
        }

    def signal_wide(sem, place):
        pl.semaphore_signal(sem, inc=1, device_id={"wide": place}, device_id_type=MESH)

    barrier = pltpu.get_barrier_semaphore()
    for offset in ((0, 0, 1), (0, 1, 0)):
        pl.semaphore_signal(barrier, inc=1, device_id=peer(*offset), device_id_type=MESH)
    has_below, has_above = z > 0, z < n_wide - 1

    @pl.when(has_below)
    def _():
        signal_wide(barrier, z - 1)

    @pl.when(has_above)
    def _():
        signal_wide(barrier, z + 1)

    loads = [
        pltpu.make_async_copy(src, dst, load_sem.at[k])
        for k, (src, dst) in enumerate(
            (
                (act_factor_hbm, act_factor),
                (padding_hbm, padding),
                (delta_factor_hbm, delta_factor),
                (delta_hbm, delta),
                (act_hbm, act),
                (assignment_hbm, assignment),
            )
        )
    ]
    for load in loads:
        load.start()

    units = block_size // UNIT
    tiles = rows // 8
    stages = tuple((0, 0, units, s * tiles // pieces, (s + 1) * tiles // pieces) for s in range(pieces))
    stages += ((1, 0, SPLIT, 0, tiles), (1, SPLIT, units, 0, tiles))

    def query_copies(stage):
        k, low, high, top, bottom = stages[stage]
        for side in (0, 1):
            first = k * pair + side * block_size + low * UNIT
            span = pl.ds(first, (high - low) * UNIT)
            part = pl.ds(8 * top, 8 * (bottom - top))
            yield pltpu.make_async_copy(
                query_hbm.at[span, part, :], query.at[span, part, :], query_sem.at[2 * stage + side]
            )

    query_starts = [copy for stage in range(len(stages)) for copy in query_copies(stage)]
    for copy in query_starts[:EARLY]:
        copy.start()

    half = act_factor.shape[1]
    pl.semaphore_wait(barrier, 2 + has_below.astype(jnp.int32) + has_above.astype(jnp.int32))

    @pl.when(has_below & has_above)
    def _():
        signal_wide(ready_sem.at[z + 1], z - 1)
        signal_wide(ready_sem.at[z - 1], z + 1)

    quarter = half // 2
    diag_copies = []
    for k, width in enumerate((quarter, half)):
        rows_at = pl.ds(pl.multiple_of(c * half + k * quarter, quarter), quarter)
        diag_copies.append(
            pltpu.make_async_remote_copy(
                src_ref=act_factor.at[rows_at, pl.ds(0, width)],
                dst_ref=diag.at[pl.ds(k * quarter, quarter), pl.ds(0, width)],
                send_sem=diag_sem.at[2 * k],
                recv_sem=diag_sem.at[2 * k + 1],
                device_id=peer(0, 1, 0),
                device_id_type=MESH,
            )
        )

    loads[0].wait()

    @pl.when(r == c)
    def _():
        for copy in diag_copies:
            copy.start()

    for load in loads[1:4]:
        load.wait()
    tokens = delta.shape[0]
    limit = 2 * tokens - padding[0] - c * tokens
    position = lax.broadcasted_iota(jnp.int32, (tokens, half), 0)
    projected = jnp.dot(delta[...], delta_factor[...], preferred_element_type=f32)
    delta_proj = jnp.where(position < limit, projected, 0.0).astype(bf16)

    loads[4].wait()
    for copy in query_starts[EARLY:]:
        copy.start()
    inner = lax.dot_general(
        delta_proj, act[...], (((0,), (0,)), ((), ())), preferred_element_type=f32
    )
    inner_copies = []
    for s in range(pieces):
        for p in range(n_wide):
            first = p * rows + s * depth
            part = inner[first : first + depth, :]
            inner_sent[s, p * depth : (p + 1) * depth, :] = part.astype(bf16)
            inner_mine[s, p * depth : (p + 1) * depth, :] = part
        copy = pltpu.make_async_remote_copy(
            src_ref=inner_sent.at[s],
            dst_ref=inner_theirs.at[s],
            send_sem=inner_send_sem.at[s],
            recv_sem=inner_recv_sem.at[s],
            device_id=peer(0, 0, 1),
            device_id_type=MESH,
        )
        copy.start()
        inner_copies.append(copy)

    for d in range(2, n_wide):

        @pl.when(z + d < n_wide)
        def _(d=d):
            pl.semaphore_wait(ready_sem.at[z + d], 1)

        @pl.when((z + d < n_wide) & has_below)
        def _(d=d):
            signal_wide(ready_sem.at[z + d], z - 1)

        @pl.when(z - d >= 0)
        def _(d=d):
            pl.semaphore_wait(ready_sem.at[z - d], 1)

        @pl.when((z - d >= 0) & has_above)
        def _(d=d):
            signal_wide(ready_sem.at[z - d], z + 1)

    near = pl.ds(pl.multiple_of(r * half, half), half)
    far = pl.ds(pl.multiple_of((1 - r) * half, half), half)

    @pl.when(r == c)
    def _():
        factor_near[...] = act_factor[near, :]

    @pl.when(r != c)
    def _():
        factor_near[...] = act_factor[far, :].astype(f32).T.astype(bf16)

    def grad_copy(s, source, place):
        target = pl.ds(pl.multiple_of(place * depth, depth), depth)
        return pltpu.make_async_remote_copy(
            src_ref=grad.at[s, target, :],
            dst_ref=grad_all.at[source, pl.ds(s * depth, depth), :],
            send_sem=grad_send_sem.at[s],
            recv_sem=grad_recv_sem.at[s],
            device_id={"wide": place},
            device_id_type=MESH,
        )

    def others():
        for step in range(n_wide - 1):
            low = n_wide - 1 - step
            yield jnp.where(2 * z < n_wide, low - (low <= z), step + (step >= z))

    def product(s, lanes, factor):
        both = inner_mine[s, :, lanes] + inner_theirs[s, :, lanes].astype(f32)
        high = both.astype(bf16)
        low = (both - high.astype(f32)).astype(bf16)
        return jnp.dot(high, factor[...], preferred_element_type=f32) + jnp.dot(
            low, factor[...], preferred_element_type=f32
        )

    for s in range(pieces):
        inner_copies[s].wait_recv()
        grad_near[s] = product(s, near, factor_near)

    @pl.when(r == c)
    def _():
        factor_far[...] = act_factor[far, :]

    @pl.when(r != c)
    def _():
        for copy in diag_copies:
            copy.wait_recv()
        factor_far[:, :quarter] = diag[:, :quarter]
        factor_far[quarter:, quarter:] = diag[quarter:, quarter:]
        factor_far[:quarter, quarter:] = diag[quarter:, :quarter].astype(f32).T.astype(bf16)

    for s in range(pieces):
        grad[s] = (grad_near[s] + product(s, far, factor_far)).astype(bf16)
        for place in others():
            grad_copy(s, z, place).start()
        own = pl.ds(pl.multiple_of(z * depth, depth), depth)
        grad_all[z, s * depth : (s + 1) * depth, :] = grad[s, own, :]

    loads[5].wait()
    stack = 8 * n_wide
    place_lane = lax.broadcasted_iota(jnp.int32, (8, stack), 1) // 8
    ranks = jnp.zeros((8, stack), jnp.int32)
    for n in range(n_wide):
        ranks = jnp.where(place_lane == n, assignment[n], ranks)
    rank_rows = lax.broadcasted_iota(jnp.int32, (8, stack), 0)
    places = jnp.where(ranks == rank_rows, 1.0, 0.0).astype(bf16)
    segments = block_size // 16
    gather = jnp.where(
        lax.broadcasted_iota(jnp.int32, (128, block_size), 0) // 8
        == lax.rem(lax.broadcasted_iota(jnp.int32, (128, block_size), 1), 16),
        1.0,
        0.0,
    ).astype(bf16)
    segment_of_lane = lax.broadcasted_iota(jnp.int32, (8, block_size), 1) // 16
    contract = (((1,), (1,)), ((), ()))

    def split(values):
        high = values.astype(bf16)
        return high, (values - high.astype(f32)).astype(bf16)

    def matches(shape, row_axis, lane_axis):
        return lax.rem(lax.broadcasted_iota(jnp.int32, shape, row_axis), 8) == lax.rem(
            lax.broadcasted_iota(jnp.int32, shape, lane_axis), 8
        )

    def weights(a):
        return grad_all[:, 8 * a : 8 * a + 8, :].reshape(stack, columns)

    def tile(start, a):
        span = pl.ds(pl.multiple_of(start, UNIT), UNIT)
        return query[span, 8 * a : 8 * a + 8, :].reshape(8 * UNIT, columns)

    def device_of(place):
        return (place["wide"] * 2 + place["rep"]) * 2 + place["sub"]

    slot = device_of(peer(0, 0, 0))

    def score_send(k, where):
        return pltpu.make_async_remote_copy(
            src_ref=outgoing.at[k, where["sub"], where["wide"]],
            dst_ref=incoming.at[slot],
            send_sem=score_send_sem,
            recv_sem=score_recv_sem,
            device_id=where,
            device_id_type=MESH,
        )

    def send_side(k, side):
        for dz in range(n_wide - 1, 0, -1):
            where = {"wide": lax.rem(z + dz, n_wide), "rep": k, "sub": side}
            score_send(k, where).start()

    def send_sibling(k):
        score_send(k, {"wide": z, "rep": k, "sub": 1 - c}).start()

    def lanes_of(u):
        return slice(8 * UNIT * u, 8 * UNIT * (u + 1))

    def rank_wide(k, chosen):
        for u in chosen:
            ranked = jnp.dot(places, wide_high[k, :, lanes_of(u)], preferred_element_type=f32)
            ranked += jnp.dot(places, wide_low[k, :, lanes_of(u)], preferred_element_type=f32)
            for g in range(UNIT // 16):
                stacked[k, u * (UNIT // 16) + g] = ranked[:, 128 * g : 128 * (g + 1)]

    def finish_wide(k):
        high, low = split(stacked[k].reshape(8 * segments, 128))
        spread = jnp.dot(high, gather, preferred_element_type=f32) + jnp.dot(
            low, gather, preferred_element_type=f32
        )
        scores = jnp.zeros((8, block_size), f32)
        for g in range(segments):
            scores = jnp.where(segment_of_lane == g, spread[8 * g : 8 * g + 8], scores)
        for p in range(n_wide):
            outgoing[k, 0, p] = scores[p : p + 1, :]
        send_side(k, 0)

    def finish_tall(k):
        high, low = split(tall_sums[k])
        scores = lax.dot_general(
            places, high, contract, preferred_element_type=f32
        ) + lax.dot_general(places, low, contract, preferred_element_type=f32)
        for p in range(n_wide):
            outgoing[k, 1, p] = scores[p : p + 1, :]
        send_side(k, 1)

    def score_stage(stage, tasks):
        for copy in query_copies(stage):
            copy.wait()
        k, low, high, top, bottom = stages[stage]
        base = k * pair
        for first in range(low, high, 2):
            group = range(first, min(high, first + 2))
            wide, tall = {}, {}
            for a in range(top, bottom):
                for u in group:
                    term = lax.dot_general(
                        weights(a), tile(base + u * UNIT, a), contract, preferred_element_type=f32
                    )
                    wide[u] = wide[u] + term if u in wide else term
                for u in group:
                    term = lax.dot_general(
                        tile(base + block_size + u * UNIT, a),
                        weights(a),
                        contract,
                        preferred_element_type=f32,
                    )
                    tall[u] = tall[u] + term if u in tall else term
            for u in group:
                if top:
                    wide[u] += total_wide[:, lanes_of(u)]
                    tall[u] += total_tall[lanes_of(u), :]
                if bottom < tiles:
                    total_wide[:, lanes_of(u)] = wide[u]
                    total_tall[lanes_of(u), :] = tall[u]
                    continue
                value = jnp.where(matches(wide[u].shape, 0, 1), wide[u], 0.0)
                wide_high[k, :, lanes_of(u)], wide_low[k, :, lanes_of(u)] = split(value)
                value = jnp.where(matches(tall[u].shape, 0, 1), tall[u], 0.0)
                tall_sums[k, UNIT * u : UNIT * (u + 1), :] = jnp.sum(
                    value.reshape(UNIT, 8, stack), axis=1
                )
            if tasks:
                tasks.pop(0)()

    def wait_grads(s):
        grads = grad.at[s, pl.ds(0, (n_wide - 1) * depth), :]
        pltpu.make_async_copy(grads, grads, grad_recv_sem.at[s]).wait()

    def first_task():
        rank_wide(0, range(units))
        finish_tall(0)

    def second_task():
        finish_wide(0)
        send_sibling(0)

    for s in range(pieces):
        wait_grads(s)
        score_stage(s, [])
    score_stage(pieces, [first_task, second_task])
    rep_copy = score_send(1 - r, peer(0, 1, 0))

    @pl.when(r == 1)
    def _():
        rep_copy.start()

    score_stage(pieces + 1, [lambda: rank_wide(1, range(SPLIT))])
    rank_wide(1, range(SPLIT, units))
    finish_tall(1)
    finish_wide(1)
    send_sibling(1)

    @pl.when(r == 0)
    def _():
        rep_copy.start()


    incoming[slot] = outgoing[r, c, z]

    @pl.when(r == c)
    def _():
        for copy in diag_copies:
            copy.wait_send()

    for copy in inner_copies:
        copy.wait_send()
    for s in range(pieces):
        grads = grad.at[s, pl.ds(0, (n_wide - 1) * depth), :]
        pltpu.make_async_copy(grads, grads, grad_send_sem.at[s]).wait()
    messages = incoming.at[pl.ds(0, 4 * n_wide - 1)]
    pltpu.make_async_copy(messages, messages, score_recv_sem).wait()
    pltpu.make_async_copy(messages, messages, score_send_sem).wait()
    out_ref[...] = jnp.sum(incoming[...], axis=0)


def fused_shards(
    n_wide, activations, deltas, act_factor, delta_factor, queries, assignment, padding
):
    _, tokens, features = activations.shape
    n_queries, rows, columns = queries.shape
    half = act_factor.shape[1]
    pieces = PIECES
    depth = rows // pieces
    block_size = n_queries // 4
    hbm = pl.BlockSpec(memory_space=pl.ANY)
    dma = pltpu.SemaphoreType.DMA
    bf16, f32 = jnp.bfloat16, jnp.float32
    return pl.pallas_call(
        functools.partial(kernel, n_wide, pieces),
        out_shape=pltpu.VMEM((1, block_size), f32),
        in_specs=[hbm] * 7,
        out_specs=pl.BlockSpec(memory_space=pltpu.VMEM),
        scratch_shapes=[
            pltpu.SMEM((n_wide,), jnp.int32),
            pltpu.SMEM((1,), jnp.int32),
            pltpu.VMEM((tokens, features), bf16),
            pltpu.VMEM((tokens, features), bf16),
            pltpu.VMEM((features, half), bf16),
            pltpu.VMEM((features, half), bf16),
            pltpu.VMEM((n_queries, rows, columns), bf16),
            pltpu.VMEM((half, half), bf16),
            pltpu.VMEM((pieces, n_wide * depth, features), f32),
            pltpu.VMEM((pieces, n_wide * depth, features), bf16),
            pltpu.VMEM((pieces, n_wide * depth, features), bf16),
            pltpu.VMEM((half, half), bf16),
            pltpu.VMEM((half, half), bf16),
            pltpu.VMEM((pieces, n_wide * depth, columns), f32),
            pltpu.VMEM((pieces, n_wide * depth, columns), bf16),
            pltpu.VMEM((n_wide, rows, columns), bf16),
            pltpu.VMEM((8 * n_wide, 8 * block_size), f32),
            pltpu.VMEM((8 * block_size, 8 * n_wide), f32),
            pltpu.VMEM((2, 8 * n_wide, 8 * block_size), bf16),
            pltpu.VMEM((2, 8 * n_wide, 8 * block_size), bf16),
            pltpu.VMEM((2, block_size // 16, 8, 128), f32),
            pltpu.VMEM((2, block_size, 8 * n_wide), f32),
            pltpu.VMEM((2, 2, n_wide, 1, block_size), f32),
            pltpu.VMEM((4 * n_wide, 1, block_size), f32),
            pltpu.SemaphoreType.REGULAR((n_wide,)),
            dma((6,)),
            dma((2 * pieces + 4,)),
            dma((4,)),
            dma((pieces,)),
            dma((pieces,)),
            dma((pieces,)),
            dma((pieces,)),
            dma,
            dma,
        ],
        compiler_params=pltpu.CompilerParams(
            collective_id=0, has_side_effects=True, vmem_limit_bytes=60 * 1024 * 1024
        ),
    )(
        assignment,
        padding,
        activations.reshape(tokens, features),
        deltas.reshape(tokens, features),
        act_factor,
        delta_factor,
        queries,
    )


def solution(mesh):
    placed = (
        P(("parts", "wide"), "sub", None),
        P(("parts", "wide"), "sub", None),
        P(None, "rep"),
        P(None, "rep"),
        P(None, ("rep", "wide"), "sub"),
        P("parts"),
        P(("parts", "wide")),
    )
    n_wide, n_rep, n_sub = (mesh.shape[name] for name in ("wide", "rep", "sub"))

    def shards(activations, deltas, act_factor, delta_factor, queries, assignment, padding):
        seq_dev, tokens, features = activations.shape
        n_queries, rows, columns = queries.shape
        fits = (
            seq_dev == 1
            and (n_rep, n_sub) == (2, 2)
            and n_wide <= 8
            and rows % (8 * PIECES) == 0
            and columns % 128 == 0
            and act_factor.shape[1] == columns == n_wide * rows
            and tokens % 16 == 0
            and n_queries % (4 * UNIT) == 0
            and n_queries * rows * columns * 2 <= 44 * 2**20
        )
        run = functools.partial(fused_shards, n_wide) if fits else general_shards
        return run(activations, deltas, act_factor, delta_factor, queries, assignment, padding)

    return jax.shard_map(
        shards,
        mesh=mesh,
        in_specs=placed,
        out_specs=P(("parts", "wide"), ("rep", "sub")),
        check_vma=False,
    )
```

time: 25.1 us -> 24.1 us (0.960)
  Pallas kernels: 23.7 us -> 22.7 us
    pallas_call x1, Pallas kernels: 23.7 us -> 22.7 us  [fused_shards(): pl.pallas_call(functools.partial(kernel, n_wide, pieces), out_shape=pltpu...]
where the time goes in v2:
time: 24.1 us; the launch traced here: 23.9 us
  Pallas kernels  22.7 us (94%)
  between operations  0.66 us (3%)
  local copies, waits for them, and re-layouts  0.56 us (2%)
    pallas_call x1, Pallas kernels, fused_shards(): pl.pallas_call(functools.partial(kernel, n_wide, pieces), out_shape=pltpu...  22.7 us
    unnamed x1, local copies, waits for them, and re-layouts  0.56 us

profile of v2, /device:TPU:3, one launch (start us, length us, event | category | flops | bytes accessed | tf_op | source)
XLA Modules:
  0.0 23.9 jit_solution(8926355800877878614)
XLA Ops:
  0.7 22.7 %shard_map.73 = f32[1,320]{1,0:T(1,128)S(1)} custom-call(s32[4]{0:T(128)} %assignment_hbm.1, s32[1]{0:T(128)S(6)} %copy.10.padding_hbm, bf16[1024,512]{1,0:T(8,128)(2,1)} %bitcast.2, bf16[1024,512]{1,0:T(8,128)(2,1)} %bitcast.3, bf16[512,256]{1,0:T(8,128)(2,1)} %act_factor_hbm.1, bf16[512,256]{1,0:T(8,128)(2,1)} %delta_factor_hbm.1, ...), custom_call_target="tpu_custom_call" | custom-call | tf_op jit(solution)/shard_map/pallas_call | solution.py:499
  23.4 0.6 %copy.9 = f32[1,320]{1,0:T(1,128)} copy(f32[1,320]{1,0:T(1,128)S(1)} %shard_map.73) | data formatting | bytes 2560

commit v3 on v2

--- a/solution.py
+++ b/solution.py
@@ -10,8 +10,10 @@
 MESH = pl.DeviceIdType.MESH
 UNIT = 32
 PIECES = 2
-EARLY = 1
+EARLY = 2
 SPLIT = 6
+DIAG_PARTS = 1
+LEAD = 4
 
 
 def general_shards(
@@ -83,9 +85,6 @@
     grad,
     grad_all,
     total_wide,
-    total_tall,
-    wide_high,
-    wide_low,
     stacked,
     tall_sums,
     outgoing,
@@ -151,18 +150,28 @@
 
     units = block_size // UNIT
     tiles = rows // 8
-    stages = tuple((0, 0, units, s * tiles // pieces, (s + 1) * tiles // pieces) for s in range(pieces))
-    stages += ((1, 0, SPLIT, 0, tiles), (1, SPLIT, units, 0, tiles))
+    cut = tiles // pieces
+    stages = (
+        ((0, 0, LEAD, 0, cut),),
+        ((0, 0, LEAD, cut, tiles), (0, LEAD, units, 0, tiles)),
+        ((1, 0, SPLIT, 0, tiles),),
+        ((1, SPLIT, units, 0, tiles),),
+    )
+    query_slots = [(stage, part) for stage in stages for part in stage]
 
     def query_copies(stage):
-        k, low, high, top, bottom = stages[stage]
-        for side in (0, 1):
-            first = k * pair + side * block_size + low * UNIT
-            span = pl.ds(first, (high - low) * UNIT)
-            part = pl.ds(8 * top, 8 * (bottom - top))
-            yield pltpu.make_async_copy(
-                query_hbm.at[span, part, :], query.at[span, part, :], query_sem.at[2 * stage + side]
-            )
+        for part in stages[stage]:
+            k, low, high, top, bottom = part
+            place = query_slots.index((stages[stage], part))
+            for side in (0, 1):
+                first = k * pair + side * block_size + low * UNIT
+                span = pl.ds(first, (high - low) * UNIT)
+                lines = pl.ds(8 * top, 8 * (bottom - top))
+                yield pltpu.make_async_copy(
+                    query_hbm.at[span, lines, :],
+                    query.at[span, lines, :],
+                    query_sem.at[2 * place + side],
+                )
 
     query_starts = [copy for stage in range(len(stages)) for copy in query_copies(stage)]
     for copy in query_starts[:EARLY]:
@@ -177,26 +186,30 @@
         signal_wide(ready_sem.at[z - 1], z + 1)
 
     quarter = half // 2
-    diag_copies = []
-    for k, width in enumerate((quarter, half)):
-        rows_at = pl.ds(pl.multiple_of(c * half + k * quarter, quarter), quarter)
-        diag_copies.append(
-            pltpu.make_async_remote_copy(
-                src_ref=act_factor.at[rows_at, pl.ds(0, width)],
-                dst_ref=diag.at[pl.ds(k * quarter, quarter), pl.ds(0, width)],
-                send_sem=diag_sem.at[2 * k],
-                recv_sem=diag_sem.at[2 * k + 1],
-                device_id=peer(0, 1, 0),
-                device_id_type=MESH,
-            )
-        )
+    piece_rows = quarter // DIAG_PARTS
+
+    def diag_copy(k):
+        width = quarter if k < DIAG_PARTS else half
+        return pltpu.make_async_remote_copy(
+            src_ref=act_factor.at[
+                pl.ds(pl.multiple_of(c * half + k * piece_rows, piece_rows), piece_rows),
+                pl.ds(0, width),
+            ],
+            dst_ref=diag.at[pl.ds(k * piece_rows, piece_rows), pl.ds(0, width)],
+            send_sem=diag_sem.at[0],
+            recv_sem=diag_sem.at[1],
+            device_id=peer(0, 1, 0),
+            device_id_type=MESH,
+        )
+
+    diag_bytes = diag.at[pl.ds(0, quarter + quarter // 2), :]
 
     loads[0].wait()
 
     @pl.when(r == c)
     def _():
-        for copy in diag_copies:
-            copy.start()
+        for k in range(2 * DIAG_PARTS):
+            diag_copy(k).start()
 
     for load in loads[1:4]:
         load.wait()
@@ -230,22 +243,18 @@
         copy.start()
         inner_copies.append(copy)
 
+    stacked[...] = jnp.zeros(stacked.shape, f32)
+
     for d in range(2, n_wide):
 
-        @pl.when(z + d < n_wide)
+        @pl.when((z + d < n_wide) & has_below)
         def _(d=d):
             pl.semaphore_wait(ready_sem.at[z + d], 1)
-
-        @pl.when((z + d < n_wide) & has_below)
-        def _(d=d):
             signal_wide(ready_sem.at[z + d], z - 1)
 
-        @pl.when(z - d >= 0)
+        @pl.when((z - d >= 0) & has_above)
         def _(d=d):
             pl.semaphore_wait(ready_sem.at[z - d], 1)
-
-        @pl.when((z - d >= 0) & has_above)
-        def _(d=d):
             signal_wide(ready_sem.at[z - d], z + 1)
 
     near = pl.ds(pl.multiple_of(r * half, half), half)
@@ -254,6 +263,7 @@
     @pl.when(r == c)
     def _():
         factor_near[...] = act_factor[near, :]
+        factor_far[...] = act_factor[far, :]
 
     @pl.when(r != c)
     def _():
@@ -283,24 +293,34 @@
             low, factor[...], preferred_element_type=f32
         )
 
-    for s in range(pieces):
-        inner_copies[s].wait_recv()
-        grad_near[s] = product(s, near, factor_near)
-
-    @pl.when(r == c)
-    def _():
-        factor_far[...] = act_factor[far, :]
+    def wait_ends():
+        @pl.when(z == 0)
+        def _():
+            for place in range(2, n_wide):
+                pl.semaphore_wait(ready_sem.at[place], 1)
+
+        @pl.when(z == n_wide - 1)
+        def _():
+            for place in range(n_wide - 2):
+                pl.semaphore_wait(ready_sem.at[place], 1)
+
+    inner_copies[0].wait_recv()
+    grad_near[...] = product(0, near, factor_near)
 
     @pl.when(r != c)
     def _():
-        for copy in diag_copies:
-            copy.wait_recv()
+        pltpu.make_async_copy(diag_bytes, diag_bytes, diag_sem.at[1]).wait()
         factor_far[:, :quarter] = diag[:, :quarter]
         factor_far[quarter:, quarter:] = diag[quarter:, quarter:]
         factor_far[:quarter, quarter:] = diag[quarter:, :quarter].astype(f32).T.astype(bf16)
 
     for s in range(pieces):
-        grad[s] = (grad_near[s] + product(s, far, factor_far)).astype(bf16)
+        if s:
+            inner_copies[s].wait_recv()
+            grad_near[...] = product(s, near, factor_near)
+        grad[s] = (grad_near[...] + product(s, far, factor_far)).astype(bf16)
+        if s == 0:
+            wait_ends()
         for place in others():
             grad_copy(s, z, place).start()
         own = pl.ds(pl.multiple_of(z * depth, depth), depth)
@@ -366,13 +386,6 @@
     def lanes_of(u):
         return slice(8 * UNIT * u, 8 * UNIT * (u + 1))
 
-    def rank_wide(k, chosen):
-        for u in chosen:
-            ranked = jnp.dot(places, wide_high[k, :, lanes_of(u)], preferred_element_type=f32)
-            ranked += jnp.dot(places, wide_low[k, :, lanes_of(u)], preferred_element_type=f32)
-            for g in range(UNIT // 16):
-                stacked[k, u * (UNIT // 16) + g] = ranked[:, 128 * g : 128 * (g + 1)]
-
     def finish_wide(k):
         high, low = split(stacked[k].reshape(8 * segments, 128))
         spread = jnp.dot(high, gather, preferred_element_type=f32) + jnp.dot(
@@ -382,7 +395,10 @@
         for g in range(segments):
             scores = jnp.where(segment_of_lane == g, spread[8 * g : 8 * g + 8], scores)
         for p in range(n_wide):
-            outgoing[k, 0, p] = scores[p : p + 1, :]
+            row = scores[0:1, :]
+            for n in range(1, n_wide):
+                row = jnp.where(assignment[n] == p, scores[n : n + 1, :], row)
+            outgoing[k, 0, p] = row
         send_side(k, 0)
 
     def finish_tall(k):
@@ -397,9 +413,11 @@
     def score_stage(stage, tasks):
         for copy in query_copies(stage):
             copy.wait()
-        k, low, high, top, bottom = stages[stage]
-        base = k * pair
-        for first in range(low, high, 2):
+        groups = [
+            (part, first) for part in stages[stage] for first in range(part[1], part[2], 2)
+        ]
+        for (k, low, high, top, bottom), first in groups:
+            base = k * pair
             group = range(first, min(high, first + 2))
             wide, tall = {}, {}
             for a in range(top, bottom):
@@ -417,19 +435,19 @@
                     )
                     tall[u] = tall[u] + term if u in tall else term
             for u in group:
+                span = slice(UNIT * u, UNIT * (u + 1))
+                value = jnp.where(matches(tall[u].shape, 0, 1), tall[u], 0.0)
+                summed = jnp.sum(value.reshape(UNIT, 8, stack), axis=1)
+                tall_sums[k, span, :] = tall_sums[k, span, :] + summed if top else summed
+                value = jnp.where(matches(wide[u].shape, 0, 1), wide[u], 0.0)
                 if top:
-                    wide[u] += total_wide[:, lanes_of(u)]
-                    tall[u] += total_tall[lanes_of(u), :]
+                    value = value + total_wide[:, lanes_of(u)]
                 if bottom < tiles:
-                    total_wide[:, lanes_of(u)] = wide[u]
-                    total_tall[lanes_of(u), :] = tall[u]
+                    total_wide[:, lanes_of(u)] = value
                     continue
-                value = jnp.where(matches(wide[u].shape, 0, 1), wide[u], 0.0)
-                wide_high[k, :, lanes_of(u)], wide_low[k, :, lanes_of(u)] = split(value)
-                value = jnp.where(matches(tall[u].shape, 0, 1), tall[u], 0.0)
-                tall_sums[k, UNIT * u : UNIT * (u + 1), :] = jnp.sum(
-                    value.reshape(UNIT, 8, stack), axis=1
-                )
+                value = jnp.sum(value.reshape(n_wide, 8, 8 * UNIT), axis=1)
+                for g in range(UNIT // 16):
+                    stacked[k, u * (UNIT // 16) + g, :n_wide, :] = value[:, 128 * g : 128 * (g + 1)]
             if tasks:
                 tasks.pop(0)()
 
@@ -438,27 +456,25 @@
         pltpu.make_async_copy(grads, grads, grad_recv_sem.at[s]).wait()
 
     def first_task():
-        rank_wide(0, range(units))
+        finish_wide(0)
         finish_tall(0)
-
-    def second_task():
-        finish_wide(0)
         send_sibling(0)
 
-    for s in range(pieces):
+    wait_grads(0)
+    score_stage(0, [])
+    for s in range(1, pieces):
         wait_grads(s)
-        score_stage(s, [])
-    score_stage(pieces, [first_task, second_task])
+    score_stage(1, [])
+    score_stage(2, [first_task])
     rep_copy = score_send(1 - r, peer(0, 1, 0))
 
     @pl.when(r == 1)
     def _():
         rep_copy.start()
 
-    score_stage(pieces + 1, [lambda: rank_wide(1, range(SPLIT))])
-    rank_wide(1, range(SPLIT, units))
+    score_stage(3, [])
+    finish_wide(1)
     finish_tall(1)
-    finish_wide(1)
     send_sibling(1)
 
     @pl.when(r == 0)
@@ -470,8 +486,7 @@
 
     @pl.when(r == c)
     def _():
-        for copy in diag_copies:
-            copy.wait_send()
+        pltpu.make_async_copy(diag_bytes, diag_bytes, diag_sem.at[0]).wait()
 
     for copy in inner_copies:
         copy.wait_send()
@@ -515,21 +530,18 @@
             pltpu.VMEM((pieces, n_wide * depth, features), bf16),
             pltpu.VMEM((half, half), bf16),
             pltpu.VMEM((half, half), bf16),
-            pltpu.VMEM((pieces, n_wide * depth, columns), f32),
+            pltpu.VMEM((n_wide * depth, columns), f32),
             pltpu.VMEM((pieces, n_wide * depth, columns), bf16),
             pltpu.VMEM((n_wide, rows, columns), bf16),
             pltpu.VMEM((8 * n_wide, 8 * block_size), f32),
-            pltpu.VMEM((8 * block_size, 8 * n_wide), f32),
-            pltpu.VMEM((2, 8 * n_wide, 8 * block_size), bf16),
-            pltpu.VMEM((2, 8 * n_wide, 8 * block_size), bf16),
             pltpu.VMEM((2, block_size // 16, 8, 128), f32),
             pltpu.VMEM((2, block_size, 8 * n_wide), f32),
             pltpu.VMEM((2, 2, n_wide, 1, block_size), f32),
             pltpu.VMEM((4 * n_wide, 1, block_size), f32),
             pltpu.SemaphoreType.REGULAR((n_wide,)),
             dma((6,)),
-            dma((2 * pieces + 4,)),
-            dma((4,)),
+            dma((10,)),
+            dma((2,)),
             dma((pieces,)),
             dma((pieces,)),
             dma((pieces,)),

time: 24.1 us -> 23.9 us (level)
  no operation moved by 1% of the time
where the time goes in v3:
time: 23.9 us; the launch traced here: 23.8 us
  Pallas kernels  22.5 us (94%)
  between operations  0.66 us (3%)
  local copies, waits for them, and re-layouts  0.56 us (2%)
    pallas_call x1, Pallas kernels, fused_shards(): pl.pallas_call(functools.partial(kernel, n_wide, pieces), out_shape=pltpu...  22.5 us
    unnamed x1, local copies, waits for them, and re-layouts  0.56 us

profile of v3, /device:TPU:3, one launch (start us, length us, event | category | flops | bytes accessed | tf_op | source)
XLA Modules:
  0.0 23.8 jit_solution(3478605934504814355)
XLA Ops:
  0.7 22.5 %shard_map.73 = f32[1,320]{1,0:T(1,128)S(1)} custom-call(s32[4]{0:T(128)} %assignment_hbm.1, s32[1]{0:T(128)S(6)} %copy.10.padding_hbm, bf16[1024,512]{1,0:T(8,128)(2,1)} %bitcast.2, bf16[1024,512]{1,0:T(8,128)(2,1)} %bitcast.3, bf16[512,256]{1,0:T(8,128)(2,1)} %act_factor_hbm.1, bf16[512,256]{1,0:T(8,128)(2,1)} %delta_factor_hbm.1, ...), custom_call_target="tpu_custom_call" | custom-call | tf_op jit(solution)/shard_map/pallas_call | solution.py:514
  23.2 0.6 %copy.9 = f32[1,320]{1,0:T(1,128)} copy(f32[1,320]{1,0:T(1,128)S(1)} %shard_map.73) | data formatting | bytes 2560

commit v4 on v3

--- a/solution.py
+++ b/solution.py
@@ -215,16 +215,16 @@
         load.wait()
     tokens = delta.shape[0]
     limit = 2 * tokens - padding[0] - c * tokens
-    position = lax.broadcasted_iota(jnp.int32, (tokens, half), 0)
-    projected = jnp.dot(delta[...], delta_factor[...], preferred_element_type=f32)
+    position = lax.broadcasted_iota(jnp.int32, (half, tokens), 1)
+    projected = lax.dot_general(
+        delta_factor[...], delta[...], (((0,), (1,)), ((), ())), preferred_element_type=f32
+    )
     delta_proj = jnp.where(position < limit, projected, 0.0).astype(bf16)
 
     loads[4].wait()
     for copy in query_starts[EARLY:]:
         copy.start()
-    inner = lax.dot_general(
-        delta_proj, act[...], (((0,), (0,)), ((), ())), preferred_element_type=f32
-    )
+    inner = jnp.dot(delta_proj, act[...], preferred_element_type=f32)
     inner_copies = []
     for s in range(pieces):
         for p in range(n_wide):
@@ -383,6 +383,11 @@
     def send_sibling(k):
         score_send(k, {"wide": z, "rep": k, "sub": 1 - c}).start()
 
+    def send_all(k):
+        send_side(k, 1)
+        send_side(k, 0)
+        send_sibling(k)
+
     def lanes_of(u):
         return slice(8 * UNIT * u, 8 * UNIT * (u + 1))
 
@@ -399,7 +404,6 @@
             for n in range(1, n_wide):
                 row = jnp.where(assignment[n] == p, scores[n : n + 1, :], row)
             outgoing[k, 0, p] = row
-        send_side(k, 0)
 
     def finish_tall(k):
         high, low = split(tall_sums[k])
@@ -408,7 +412,6 @@
         ) + lax.dot_general(places, low, contract, preferred_element_type=f32)
         for p in range(n_wide):
             outgoing[k, 1, p] = scores[p : p + 1, :]
-        send_side(k, 1)
 
     def score_stage(stage, tasks):
         for copy in query_copies(stage):
@@ -456,9 +459,9 @@
         pltpu.make_async_copy(grads, grads, grad_recv_sem.at[s]).wait()
 
     def first_task():
+        finish_tall(0)
         finish_wide(0)
-        finish_tall(0)
-        send_sibling(0)
+        send_all(0)
 
     wait_grads(0)
     score_stage(0, [])
@@ -473,9 +476,9 @@
         rep_copy.start()
 
     score_stage(3, [])
+    finish_tall(1)
     finish_wide(1)
-    finish_tall(1)
-    send_sibling(1)
+    send_all(1)
 
     @pl.when(r == 0)
     def _():
@@ -495,8 +498,8 @@
         pltpu.make_async_copy(grads, grads, grad_send_sem.at[s]).wait()
     messages = incoming.at[pl.ds(0, 4 * n_wide - 1)]
     pltpu.make_async_copy(messages, messages, score_recv_sem).wait()
+    out_ref[...] = jnp.sum(incoming[...], axis=0)
     pltpu.make_async_copy(messages, messages, score_send_sem).wait()
-    out_ref[...] = jnp.sum(incoming[...], axis=0)
 
 
 def fused_shards(

time: 23.9 us -> 23.6 us (0.987)
  Pallas kernels: 22.5 us -> 22.2 us
    pallas_call x1, Pallas kernels: 22.5 us -> 22.2 us  [fused_shards(): pl.pallas_call(functools.partial(kernel, n_wide, pieces), out_shape=pltpu...]
where the time goes in v4:
time: 23.6 us; the launch traced here: 23.4 us
  Pallas kernels  22.2 us (94%)
  between operations  0.66 us (3%)
  local copies, waits for them, and re-layouts  0.56 us (2%)
    pallas_call x1, Pallas kernels, fused_shards(): pl.pallas_call(functools.partial(kernel, n_wide, pieces), out_shape=pltpu...  22.2 us
    unnamed x1, local copies, waits for them, and re-layouts  0.56 us

profile of v4, /device:TPU:3, one launch (start us, length us, event | category | flops | bytes accessed | tf_op | source)
XLA Modules:
  0.0 23.4 jit_solution(3264886460970246849)
XLA Ops:
  0.7 22.2 %shard_map.73 = f32[1,320]{1,0:T(1,128)S(1)} custom-call(s32[4]{0:T(128)} %assignment_hbm.1, s32[1]{0:T(128)S(6)} %copy.10.padding_hbm, bf16[1024,512]{1,0:T(8,128)(2,1)} %bitcast.2, bf16[1024,512]{1,0:T(8,128)(2,1)} %bitcast.3, bf16[512,256]{1,0:T(8,128)(2,1)} %act_factor_hbm.1, bf16[512,256]{1,0:T(8,128)(2,1)} %delta_factor_hbm.1, ...), custom_call_target="tpu_custom_call" | custom-call | tf_op jit(solution)/shard_map/pallas_call | solution.py:517
  22.9 0.6 %copy.9 = f32[1,320]{1,0:T(1,128)} copy(f32[1,320]{1,0:T(1,128)S(1)} %shard_map.73) | data formatting | bytes 2560

commit v5 on v4

--- a/solution.py
+++ b/solution.py
@@ -376,9 +376,8 @@
         )
 
     def send_side(k, side):
-        for dz in range(n_wide - 1, 0, -1):
-            where = {"wide": lax.rem(z + dz, n_wide), "rep": k, "sub": side}
-            score_send(k, where).start()
+        for place in others():
+            score_send(k, {"wide": place, "rep": k, "sub": side}).start()
 
     def send_sibling(k):
         score_send(k, {"wide": z, "rep": k, "sub": 1 - c}).start()

time: 23.6 us -> 23.6 us (level)
  no operation moved by 1% of the time
where the time goes in v5:
time: 23.6 us; the launch traced here: 23.4 us
  Pallas kernels  22.2 us (94%)
  between operations  0.66 us (3%)
  local copies, waits for them, and re-layouts  0.56 us (2%)
    pallas_call x1, Pallas kernels, fused_shards(): pl.pallas_call(functools.partial(kernel, n_wide, pieces), out_shape=pltpu...  22.2 us
    unnamed x1, local copies, waits for them, and re-layouts  0.56 us

profile of v5, /device:TPU:3, one launch (start us, length us, event | category | flops | bytes accessed | tf_op | source)
XLA Modules:
  0.0 23.4 jit_solution(13296725124778228131)
XLA Ops:
  0.7 22.2 %shard_map.73 = f32[1,320]{1,0:T(1,128)S(1)} custom-call(s32[4]{0:T(128)} %assignment_hbm.1, s32[1]{0:T(128)S(6)} %copy.10.padding_hbm, bf16[1024,512]{1,0:T(8,128)(2,1)} %bitcast.2, bf16[1024,512]{1,0:T(8,128)(2,1)} %bitcast.3, bf16[512,256]{1,0:T(8,128)(2,1)} %act_factor_hbm.1, bf16[512,256]{1,0:T(8,128)(2,1)} %delta_factor_hbm.1, ...), custom_call_target="tpu_custom_call" | custom-call | tf_op jit(solution)/shard_map/pallas_call | solution.py:516
  22.9 0.6 %copy.9 = f32[1,320]{1,0:T(1,128)} copy(f32[1,320]{1,0:T(1,128)S(1)} %shard_map.73) | data formatting | bytes 2560
